TPU v7x, 32 devices: a whole 2x2x4 slice. The times are simulated.
32 devices in a mesh: groups: 2 (over y), freq: 16 (over z, x, core).
Axes of the slice: x: 2, y: 2, z: 4, core: 2. Of those that a mesh axis runs over, the one named last changes fastest.
Arguments:
- refl: bfloat16 [128, 2, 512, 512], P(('groups', 'freq')), parts along dimension 0, may hold values from -0.1875 to 0.1875
- refl_scale: float32 [128, 4], P(('groups', 'freq')), parts along dimension 0, may hold values from 0.5 to 4
- freq_index: int32 [128], P(('groups', 'freq')), parts along dimension 0, may hold values from 1 to 1023, as said below
- fd_plus: bfloat16 [4096, 32, 512], P(('groups', 'freq')), parts along dimension 0, may hold values from -6 to 6
- onset: int32 [32768], P(('groups', 'freq')), parts along dimension 0, may hold values from 128 to 767
Outputs:
- f_minus: bfloat16 [4096, 32, 512], P(('groups', 'freq')), parts along dimension 0
- f_plus: float32 [4096, 32, 512], P(('groups', 'freq')), parts along dimension 0
There are 2 independent parts, one for each index of `groups`. A program takes and returns all parts, laid end to end along the dimension named above; each array names one. Nothing has to cross between parts.
Inputs may be any that keep to these rules, and one draw needn't show every extreme that they name: `freq_index`: the bins are distinct and ascending; the first is 1 and the last is 1023.
All inputs are finite; a program needn't handle non-finite values.
Results may differ from a plain program's by a relative error of at most 0.01.
Values may be sent and summed in bfloat16 or wider, within the bound.
No kernel may reach another device: no remote copies, remote signals or barrier semaphores. Data moves between devices by JAX's collectives and lax.ppermute only.
A program may use at most 128 MiB of HBM per device.

v0:
```python
import math
import jax
import jax.numpy as jnp
from jax import lax
from jax.sharding import PartitionSpec as P


def to_columns(field):
    return lax.all_to_all(field, "freq", split_axis=1, concat_axis=0, tiled=True)


def to_time(field):
    return lax.all_to_all(field, "freq", split_axis=0, concat_axis=1, tiled=True)


def local(refl, refl_scale, freq_index, fd_plus, onset):
    nfreq_dev = refl.shape[0]
    nrec = refl.shape[2]
    t_dev, points, _ = fd_plus.shape
    columns = points * nrec
    nshard = lax.axis_size("freq")
    ntime = t_dev * nshard
    width = columns // nshard
    first_col = lax.axis_index("freq") * width
    bins, scales = (
        lax.all_gather(freq_index, "freq", axis=0, tiled=True),
        lax.all_gather(refl_scale, "freq", axis=0, tiled=True),
    )
    nblocks = scales.shape[1]
    times = jnp.arange(ntime, dtype=jnp.int32)
    phase = bins[:, None] * times[None, :] % ntime
    angle = phase.astype(jnp.float32) * jnp.float32(2.0 * math.pi / ntime)
    cosine = jnp.cos(angle).astype(jnp.bfloat16)
    sine = jnp.sin(angle).astype(jnp.bfloat16)
    col_ids = first_col + jnp.arange(width, dtype=jnp.int32)
    block_ids = col_ids % nrec // (nrec // nblocks)
    onehot = (block_ids[None, :] == jnp.arange(nblocks, dtype=jnp.int32)[:, None]).astype(
        jnp.float32
    )
    col_scale = jnp.dot(
        scales, onehot, precision=lax.Precision.HIGHEST, preferred_element_type=jnp.float32
    )
    signed = jnp.where(times < ntime // 2, times, times - ntime)
    keep = (jnp.abs(signed)[:, None] < onset[None, :]).astype(jnp.float32)
    contract_time = (((0,), (0,)), ((), ()))

    def forward(colfield, table_c, table_s):
        real = jnp.dot(table_c, colfield, preferred_element_type=jnp.float32)
        imag = -jnp.dot(table_s, colfield, preferred_element_type=jnp.float32)
        spectrum = jnp.stack(
            [(real * col_scale).astype(jnp.bfloat16), (imag * col_scale).astype(jnp.bfloat16)],
            axis=1,
        )
        return lax.all_to_all(spectrum, "freq", split_axis=0, concat_axis=2, tiled=True)

    def convolve(spectrum, sign):
        spectrum = spectrum.reshape(nfreq_dev, 2, points, nrec)
        spec_r = spectrum[:, 0]
        spec_i = spectrum[:, 1]
        resp_r = refl[:, 0]
        resp_i = refl[:, 1]

        def apply(resp, spec):
            return jnp.einsum("frs,fvs->fvr", resp, spec, preferred_element_type=jnp.float32)

        out_r = apply(resp_r, spec_r) - sign * apply(resp_i, spec_i)
        out_i = apply(resp_r, spec_i) + sign * apply(resp_i, spec_r)
        stacked = jnp.stack([out_r.astype(jnp.bfloat16), out_i.astype(jnp.bfloat16)], axis=1)
        return lax.all_to_all(
            stacked.reshape(nfreq_dev, 2, columns), "freq", split_axis=2, concat_axis=0, tiled=True
        )

    def inverse(spectrum):
        trace = lax.dot_general(
            cosine, spectrum[:, 0], contract_time, preferred_element_type=jnp.float32
        )
        trace = trace - lax.dot_general(
            sine, spectrum[:, 1], contract_time, preferred_element_type=jnp.float32
        )
        return (trace * jnp.float32(2.0 / ntime) * keep).astype(jnp.bfloat16)

    direct = fd_plus.reshape(t_dev, columns)
    minus_cols = inverse(convolve(forward(to_columns(direct), cosine, sine), 1.0))
    minus_time = to_time(minus_cols)
    update_cols = inverse(convolve(forward(minus_cols, cosine, sine), -1.0))
    plus_time = direct.astype(jnp.float32) + to_time(update_cols).astype(jnp.float32)
    return (minus_time.reshape(t_dev, points, nrec), plus_time.reshape(t_dev, points, nrec))


def solution(mesh):
    return jax.shard_map(
        local,
        mesh=mesh,
        in_specs=(
            P(("groups", "freq"), None, None, None),
            P(("groups", "freq"), None),
            P(("groups", "freq")),
            P(("groups", "freq"), None, None),
            P(("groups", "freq")),
        ),
        out_specs=(P(("groups", "freq"), None, None), P(("groups", "freq"), None, None)),
        check_vma=False,
    )
```

profile of v0, /device:TPU:11, one launch (start us, length us, event | category | flops | bytes accessed | tf_op | source)
XLA Modules:
  0.0 541.2 jit_solution(8030469073627968279)
XLA Ops:
  0.6 7.9 %copy.51 = bf16[128,32,512]{0,2,1:T(8,128)(2,1)} copy(bf16[128,32,512]{2,1,0:T(8,128)(2,1)} %param.8) | data formatting | bytes 8388608 | tf_op args[3]
  8.5 6.7 %all-to-all-start = ((bf16[128,16,1024]{0,2,1:T(8,128)(2,1)}), bf16[128,16,1024]{0,2,1:T(8,128)(2,1)}, u32[]{:S(2)}, u32[]{:S(2)}) async-start(bf16[128,16,1024]{0,2,1:T(8,128)(2,1)} %bitcast.126), calls=%async_computation | async-start | bytes 8388608 | tf_op jit(solution)/shard_map/all_to_all | solution.py:9
  15.2 0.6 dynamic-slice
  16.5 0.2 dynamic-update-slice
  16.7 88.9 %all-reduce = s32[64]{0:T(128)S(1)} all-reduce(s32[64]{0:T(128)S(1)} %dynamic-update-slice), channel_id=1, replica_groups=mesh['groups'=2,'freq'=16] {'freq'}, use_global_device_ids=true, to_apply=%add | all-reduce | flops 64 | bytes 512
  105.6 18.6 %all-gather = f32[16,4,4]{2,1,0:T(4,128)S(1)} all-gather(f32[1,4,4]{2,1,0:T(4,128)S(1)} %bitcast.140), channel_id=1, replica_groups=mesh['groups'=2,'freq'=16] {'freq'}, dimensions={0}, use_global_device_ids=true | all-gather | bytes 1088 | tf_op jit(solution)/shard_map/all_gather | solution.py:27
  124.2 0.2 convolution_bitcast_fusion
  124.5 6.4 %copy.52 = bf16[16,128,1024]{2,1,0:T(8,128)(2,1)} copy(bf16[16,128,1024]{1,2,0:T(8,128)(2,1)} %bitcast.2) | data formatting | bytes 8388608 | tf_op jit(solution)/shard_map/all_to_all | solution.py:9
  130.9 4.5 fusion.64
  135.4 2.5 fusion.65
  138.0 0.3 copy.53
  138.2 15.2 %all_to_all.114 = bf16[64,2,1024]{2,1,0:T(2,128)(2,1)S(1)} all-to-all(bf16[64,2,1024]{2,1,0:T(2,128)(2,1)S(1)} %copy.53), channel_id=1, replica_groups=mesh['groups'=2,'freq'=16] {'freq'}, dimensions={0} | all-to-all | bytes 524288 | tf_op jit(solution)/shard_map/all_to_all | solution.py:54
  153.4 0.1 copy.94
  153.6 0.1 reshape.82
  153.7 2.4 fusion.6
  156.2 2.3 fusion.8
  158.5 0.7 fusion.56
  159.2 0.1 stack.40
  159.3 2.3 fusion.59
  161.6 0.1 stack.39
  161.7 0.2 pad_maximum_fusion.1
  161.9 13.0 %copy.57 = bf16[4,2,16384]{0,1,2:T(2,128)(2,1)} copy(bf16[4,2,16384]{2,0,1:T(4,128)(2,1)S(1)} %pad_maximum_fusion.1) | data formatting | bytes 524288 | tf_op jit(solution)/shard_map/stack | solution.py:68
  174.9 16.8 %reshape.93 = bf16[16,2,4096]{2,1,0:T(2,128)(2,1)} reshape(bf16[16384,2,4]{2,1,0:T(2,128)(2,1)} %bitcast.122) | data formatting | bytes 524288
  191.7 6.1 %all-to-all-start.2 = ((bf16[16,2,4096]{2,1,0:T(2,128)(2,1)}), bf16[16,2,4096]{2,1,0:T(2,128)(2,1)S(1)}, u32[]{:S(2)}, u32[]{:S(2)}) async-start(bf16[16,2,4096]{2,1,0:T(2,128)(2,1)} %reshape.93), calls=%async_computation.2 | async-start | bytes 524288 | tf_op jit(solution)/shard_map/all_to_all | solution.py:69
  197.8 7.9 %all-to-all-done.2 = bf16[16,2,4096]{2,1,0:T(2,128)(2,1)S(1)} async-done(((bf16[16,2,4096]{2,1,0:T(2,128)(2,1)}), bf16[16,2,4096]{2,1,0:T(2,128)(2,1)S(1)}, u32[]{:S(2)}, u32[]{:S(2)}) %all-to-all-start.2) | async-done | bytes 262176 | tf_op jit(solution)/shard_map/all_to_all | solution.py:69
  205.7 19.0 %reshape.94 = bf16[16384,2,4]{2,1,0:T(2,128)(2,1)} reshape(bf16[16,2,4096]{2,1,0:T(2,128)(2,1)S(1)} %all-to-all-done.2) | data formatting | bytes 524288
  224.7 11.9 %copy.67 = bf16[4,2,16,1024]{3,2,1,0:T(8,128)(2,1)S(1)} copy(bf16[4,2,16,1024]{0,1,3,2:T(2,128)(2,1)} %bitcast.123) | data formatting | bytes 524288 | tf_op jit(solution)/shard_map/all_to_all | solution.py:69
  236.6 0.3 copy.59
  236.9 0.4 fusion.123
  237.3 3.1 fusion.73
  240.4 4.1 fusion
  244.5 2.5 fusion.62
  247.1 2.5 fusion.63
  249.6 0.3 copy.61
  249.9 13.0 %all_to_all.115 = bf16[64,2,1024]{2,1,0:T(2,128)(2,1)S(1)} all-to-all(bf16[64,2,1024]{2,1,0:T(2,128)(2,1)S(1)} %copy.61), channel_id=1, replica_groups=mesh['groups'=2,'freq'=16] {'freq'}, dimensions={0} | all-to-all | bytes 524288 | tf_op jit(solution)/shard_map/all_to_all | solution.py:54
  262.9 0.1 copy.93
  263.1 0.1 reshape.84
  263.2 2.5 fusion.41
  265.7 2.3 fusion.38
  268.0 0.0 copy-done.1
  268.0 0.7 fusion.50
  268.7 0.1 stack.46
  268.8 2.3 fusion.53
  271.1 0.1 stack.45
  271.2 0.2 pad_maximum_fusion.3
  271.4 13.0 %copy.63 = bf16[4,2,16384]{0,1,2:T(2,128)(2,1)} copy(bf16[4,2,16384]{2,0,1:T(4,128)(2,1)S(1)} %pad_maximum_fusion.3) | data formatting | bytes 524288 | tf_op jit(solution)/shard_map/stack | solution.py:68
  284.4 16.2 %reshape.95 = bf16[16,2,4096]{2,1,0:T(2,128)(2,1)S(1)} reshape(bf16[16384,2,4]{2,1,0:T(2,128)(2,1)} %bitcast.124) | data formatting | bytes 524288
  300.6 12.8 %all_to_all.116 = bf16[16,2,4096]{2,1,0:T(2,128)(2,1)S(1)} all-to-all(bf16[16,2,4096]{2,1,0:T(2,128)(2,1)S(1)} %reshape.95), channel_id=1, replica_groups=mesh['groups'=2,'freq'=16] {'freq'}, dimensions={0} | all-to-all | bytes 524288 | tf_op jit(solution)/shard_map/all_to_all | solution.py:69
  313.4 6.5 %all-to-all-start.3 = ((bf16[16,128,1024]{2,1,0:T(8,128)(2,1)}), bf16[16,128,1024]{2,1,0:T(8,128)(2,1)}, u32[]{:S(2)}, u32[]{:S(2)}) async-start(bf16[16,128,1024]{2,1,0:T(8,128)(2,1)} %bitcast.127), calls=%async_computation.3 | async-start | bytes 8388608 | tf_op jit(solution)/shard_map/all_to_all | solution.py:13
  319.9 19.1 %reshape.96 = bf16[16384,2,4]{2,1,0:T(2,128)(2,1)} reshape(bf16[16,2,4096]{2,1,0:T(2,128)(2,1)S(1)} %all_to_all.116) | data formatting | bytes 524288
  338.9 11.9 %copy.68 = bf16[4,2,16,1024]{3,2,1,0:T(8,128)(2,1)S(1)} copy(bf16[4,2,16,1024]{0,1,3,2:T(2,128)(2,1)} %bitcast.125) | data formatting | bytes 524288 | tf_op jit(solution)/shard_map/all_to_all | solution.py:69
  350.8 0.3 copy.65
  351.1 0.4 fusion.122
  351.5 3.1 fusion.72
  354.6 4.9 fusion.1
  359.5 52.8 %all-to-all-done.3 = bf16[16,128,1024]{2,1,0:T(8,128)(2,1)} async-done(((bf16[16,128,1024]{2,1,0:T(8,128)(2,1)}), bf16[16,128,1024]{2,1,0:T(8,128)(2,1)}, u32[]{:S(2)}, u32[]{:S(2)}) %all-to-all-start.3) | async-done | bytes 4194336 | tf_op jit(solution)/shard_map/all_to_all | solution.py:13
  412.4 5.2 all-to-all-start.6
  417.6 6.5 %copy.60 = bf16[128,16,1024]{2,1,0:T(8,128)(2,1)} copy(bf16[128,16,1024]{2,0,1:T(8,128)(2,1)} %bitcast.19) | data formatting | bytes 8388608 | tf_op jit(solution)/shard_map/all_to_all | solution.py:13
  424.1 7.1 %reshape.83 = bf16[128,32,512]{2,1,0:T(8,128)(2,1)} reshape(bf16[128,16,1024]{2,1,0:T(8,128)(2,1)} %copy.60) | data formatting | bytes 8388608 | tf_op jit(solution)/shard_map/reshape | solution.py:87
  431.2 78.7 %all-to-all-done.6 = bf16[16,128,1024]{2,1,0:T(8,128)(2,1)} async-done(((bf16[16,128,1024]{2,1,0:T(8,128)(2,1)}), bf16[16,128,1024]{2,1,0:T(8,128)(2,1)}, u32[]{:S(2)}, u32[]{:S(2)}) %all-to-all-start.6) | async-done | bytes 4194336 | tf_op jit(solution)/shard_map/all_to_all | solution.py:13
  509.9 3.2 convert_bitcast_fusion
  513.2 8.3 %copy.66 = f32[128,16,1024]{2,1,0:T(8,128)} copy(f32[128,16,1024]{2,0,1:T(8,128)S(1)} %convert_bitcast_fusion) | data formatting | bytes 16777216 | tf_op jit(solution)/shard_map/convert_element_type | solution.py:86
  521.4 9.3 %reshape.85 = f32[128,32,512]{2,1,0:T(8,128)} reshape(f32[128,16,1024]{2,1,0:T(8,128)} %copy.66) | data formatting | bytes 16777216 | tf_op jit(solution)/shard_map/convert_element_type | solution.py:86
  530.7 10.2 %convert_add_fusion = f32[128,32,512]{2,1,0:T(8,128)} fusion(f32[128,32,512]{2,1,0:T(8,128)} %reshape.85, bf16[128,32,512]{2,1,0:T(8,128)(2,1)} %param.8), kind=kLoop, calls=%fused_computation.5 | loop fusion | flops 4194304 | bytes 20971520 | tf_op jit(solution)/shard_map/add | solution.py:86
  (21 shorter events, 0.1 us)
Async XLA Ops:
  8.5 6.7 %copy-start.7 = (u32[32]{0:T(128)S(1)}, u32[32]{0:T(128)}, u32[]{:S(2)}) copy-start(u32[32]{0:T(128)} %constant.68) | copy-start | bytes 388
  8.5 8.0 %copy-start.6 = (s32[4]{0:T(128)S(1)}, s32[4]{0:T(128)}, u32[]{:S(2)}) copy-start(s32[4]{0:T(128)} %param.7) | copy-start | bytes 52
  8.5 97.1 %copy-start.4 = (f32[4,4]{1,0:T(4,128)S(1)}, f32[4,4]{1,0:T(4,128)}, u32[]{:S(2)}) copy-start(f32[4,4]{1,0:T(4,128)} %param.6) | copy-start | bytes 196
  8.5 115.9 %all-to-all-start = ((bf16[128,16,1024]{0,2,1:T(8,128)(2,1)}), bf16[128,16,1024]{0,2,1:T(8,128)(2,1)}, u32[]{:S(2)}, u32[]{:S(2)}) async-start(bf16[128,16,1024]{0,2,1:T(8,128)(2,1)} %bitcast.126), calls=%async_computation | async-start | bytes 8388608 | tf_op jit(solution)/shard_map/all_to_all | solution.py:9
  130.9 4.5 copy-start.3
  153.7 4.8 copy-start
  191.7 14.0 %all-to-all-start.2 = ((bf16[16,2,4096]{2,1,0:T(2,128)(2,1)}), bf16[16,2,4096]{2,1,0:T(2,128)(2,1)S(1)}, u32[]{:S(2)}, u32[]{:S(2)}) async-start(bf16[16,2,4096]{2,1,0:T(2,128)(2,1)} %reshape.93), calls=%async_computation.2 | async-start | bytes 524288 | tf_op jit(solution)/shard_map/all_to_all | solution.py:69
  237.3 3.1 copy-start.5
  244.5 5.1 copy-start.2
  263.2 4.8 copy-start.1
  313.4 99.0 %all-to-all-start.3 = ((bf16[16,128,1024]{2,1,0:T(8,128)(2,1)}), bf16[16,128,1024]{2,1,0:T(8,128)(2,1)}, u32[]{:S(2)}, u32[]{:S(2)}) async-start(bf16[16,128,1024]{2,1,0:T(8,128)(2,1)} %bitcast.127), calls=%async_computation.3 | async-start | bytes 8388608 | tf_op jit(solution)/shard_map/all_to_all | solution.py:13
  412.4 97.6 %all-to-all-start.6 = ((bf16[16,128,1024]{2,1,0:T(8,128)(2,1)}), bf16[16,128,1024]{2,1,0:T(8,128)(2,1)}, u32[]{:S(2)}, u32[]{:S(2)}) async-start(bf16[16,128,1024]{2,1,0:T(8,128)(2,1)} %bitcast.128), calls=%async_computation.6 | async-start | bytes 8388608 | tf_op jit(solution)/shard_map/all_to_all | solution.py:13
where the time goes:
time: 550 us; the launch traced here: 541 us
  local copies, waits for them, and re-layouts  170 us (31%)
  blocking collectives  149 us (27%)
  waiting for transfers between devices  139 us (25%)
  matrix products  43.1 us (8%)
  starting transfers between devices  24.6 us (4%)
  other arithmetic  13.8 us (3%)
    all_to_all x2, waiting for transfers between devices, to_time(): lax.all_to_all(field, 'freq', split_axis=0, concat_axis=1, tiled=True)  132 us
    unnamed x1, blocking collectives  88.9 us
    unnamed x24, local copies, waits for them, and re-layouts  79.9 us
    all_to_all x2, blocking collectives, forward(): lax.all_to_all(spectrum, 'freq', split_axis=0, concat_axis=2, tiled=True)  28.2 us
    another operation x6, local copies, waits for them, and re-layouts, convolve(): jnp.stack([out_r.astype(jnp.bfloat16), out_i.astype(jnp.bfloat16)], axis=1)  26.2 us
    all_to_all x4, local copies, waits for them, and re-layouts, convolve(): lax.all_to_all(stacked.reshape(nfreq_dev, 2, columns), 'freq', split_axis...  24.3 us
    all_gather x1, blocking collectives, local(): lax.all_gather(refl_scale, 'freq', axis=0, tiled=True)  18.6 us
    convert_element_type x2, local copies, waits for them, and re-layouts, local(): to_time(update_cols).astype(jnp.float32)  17.6 us
  transfers between devices with their start and end apart: 4, of which 3 were waited for; matrix products, arithmetic and copies ran while one was open for 10% of the time, Pallas kernels for 0%

commit v1 on v0

--- a/solution.py
+++ b/solution.py
@@ -3,6 +3,28 @@
 import jax.numpy as jnp
 from jax import lax
 from jax.sharding import PartitionSpec as P
+
+
+def in_order(blocks, dim):
+    blocks = jnp.moveaxis(blocks, 0, dim)
+    shape = blocks.shape
+    return blocks.reshape(*shape[:dim], shape[dim] * shape[dim + 1], *shape[dim + 2 :])
+
+
+def doubled(array, axis):
+    size = lax.axis_size(axis)
+    parts = array[None]
+    for level in range(size.bit_length() - 1):
+        stride = 1 << level
+        theirs = lax.ppermute(parts, axis, [(i, i ^ stride) for i in range(size)])
+        both = jnp.stack([parts, theirs])
+        upper = lax.axis_index(axis) >> level & 1
+        parts = jnp.where(upper == 0, both, both[::-1]).reshape(-1, *array.shape)
+    return parts
+
+
+def gather_by_bits(x, axis, dim):
+    return in_order(doubled(x, axis), dim)
 
 
 def to_columns(field):
@@ -24,7 +46,7 @@
     first_col = lax.axis_index("freq") * width
     bins, scales = (
         lax.all_gather(freq_index, "freq", axis=0, tiled=True),
-        lax.all_gather(refl_scale, "freq", axis=0, tiled=True),
+        gather_by_bits(refl_scale, "freq", 0),
     )
     nblocks = scales.shape[1]
     times = jnp.arange(ntime, dtype=jnp.int32)

time: 550 us -> 533 us (0.969)
  blocking collectives: 149 us -> 59.2 us
  waiting for transfers between devices: 139 us -> 209 us
    unnamed x1, blocking collectives: 88.9 us -> 19.5 us
    ppermute x0 -> x4, waiting for transfers between devices: none -> 68.3 us  [doubled(): theirs = lax.ppermute(parts, axis, [(i, i ^ stride) for i in range(size)])]
    all_gather x1 -> x0, blocking collectives: 18.6 us -> none  [local(): lax.all_gather(refl_scale, 'freq', axis=0, tiled=True)]
  transfers between devices with their start and end apart: 4 -> 8, of which waited for: 3 -> 7; matrix products, arithmetic and copies ran while one was open for 10% -> 10% of each run, Pallas kernels for 0% -> 0%
where the time goes in v1:
time: 533 us; the launch traced here: 523 us
  waiting for transfers between devices  209 us (39%)
  local copies, waits for them, and re-layouts  170 us (32%)
  blocking collectives  59.2 us (11%)
  matrix products  43.2 us (8%)
  starting transfers between devices  25.8 us (5%)
  other arithmetic  13.9 us (3%)
    all_to_all x2, waiting for transfers between devices, to_time(): lax.all_to_all(field, 'freq', split_axis=0, concat_axis=1, tiled=True)  132 us
    unnamed x24, local copies, waits for them, and re-layouts  79.9 us
    ppermute x4, waiting for transfers between devices, doubled(): theirs = lax.ppermute(parts, axis, [(i, i ^ stride) for i in range(size)])  68.3 us
    all_to_all x2, blocking collectives, forward(): lax.all_to_all(spectrum, 'freq', split_axis=0, concat_axis=2, tiled=True)  26.9 us
    another operation x6, local copies, waits for them, and re-layouts, convolve(): jnp.stack([out_r.astype(jnp.bfloat16), out_i.astype(jnp.bfloat16)], axis=1)  26.2 us
    all_to_all x4, local copies, waits for them, and re-layouts, convolve(): lax.all_to_all(stacked.reshape(nfreq_dev, 2, columns), 'freq', split_axis...  24.3 us
    unnamed x1, blocking collectives  19.5 us
    convert_element_type x2, local copies, waits for them, and re-layouts, local(): to_time(update_cols).astype(jnp.float32)  17.6 us
  transfers between devices with their start and end apart: 8, of which 7 were waited for; matrix products, arithmetic and copies ran while one was open for 10% of the time, Pallas kernels for 0%

profile of v1, /device:TPU:11, one launch (start us, length us, event | category | flops | bytes accessed | tf_op | source)
XLA Modules:
  0.0 523.4 jit_solution(2789555168285376598)
XLA Ops:
  0.6 7.9 %copy.62 = bf16[128,32,512]{0,2,1:T(8,128)(2,1)} copy(bf16[128,32,512]{2,1,0:T(8,128)(2,1)} %param.8) | data formatting | bytes 8388608 | tf_op args[3]
  8.5 6.7 %all-to-all-start = ((bf16[128,16,1024]{0,2,1:T(8,128)(2,1)}), bf16[128,16,1024]{0,2,1:T(8,128)(2,1)}, u32[]{:S(2)}, u32[]{:S(2)}) async-start(bf16[128,16,1024]{0,2,1:T(8,128)(2,1)} %bitcast.140), calls=%async_computation | async-start | bytes 8388608 | tf_op jit(solution)/shard_map/all_to_all | solution.py:31
  15.2 0.4 collective-permute-start
  15.7 0.9 collective-permute-done
  16.6 0.3 collective-permute-start.1
  16.9 16.6 %collective-permute-done.1 = f32[2,4,4]{2,1,0:T(4,128)S(1)} collective-permute-done((f32[2,4,4]{2,1,0:T(4,128)S(1)}, f32[2,4,4]{2,1,0:T(4,128)S(1)}, u32[]{:S(2)}, u32[]{:S(2)}) %collective-permute-start.1) | collective-permute-done | bytes 160 | tf_op jit(solution)/shard_map/ppermute | solution.py:19
  33.5 0.4 collective-permute-start.2
  33.9 0.6 dynamic-slice
  34.5 50.8 %collective-permute-done.2 = f32[4,4,4]{2,1,0:T(4,128)S(1)} collective-permute-done((f32[4,4,4]{2,1,0:T(4,128)S(1)}, f32[4,4,4]{2,1,0:T(4,128)S(1)}, u32[]{:S(2)}, u32[]{:S(2)}) %collective-permute-start.2) | collective-permute-done | bytes 288 | tf_op jit(solution)/shard_map/ppermute | solution.py:19
  86.2 0.2 dynamic-update-slice
  86.4 19.5 %all-reduce = s32[64]{0:T(128)S(1)} all-reduce(s32[64]{0:T(128)S(1)} %dynamic-update-slice), channel_id=1, replica_groups=mesh['groups'=2,'freq'=16] {'freq'}, use_global_device_ids=true, to_apply=%add | all-reduce | flops 64 | bytes 512
  106.1 0.1 copy.66
  106.3 0.3 fusion.82
  106.6 1.5 all-to-all-done
  108.1 6.4 %copy.63 = bf16[16,128,1024]{2,1,0:T(8,128)(2,1)} copy(bf16[16,128,1024]{1,2,0:T(8,128)(2,1)} %bitcast.2) | data formatting | bytes 8388608 | tf_op jit(solution)/shard_map/all_to_all | solution.py:31
  114.5 4.5 fusion.64
  119.0 2.5 fusion.65
  121.6 0.3 copy.67
  121.9 13.8 %all_to_all.114 = bf16[64,2,1024]{2,1,0:T(2,128)(2,1)S(1)} all-to-all(bf16[64,2,1024]{2,1,0:T(2,128)(2,1)S(1)} %copy.67), channel_id=1, replica_groups=mesh['groups'=2,'freq'=16] {'freq'}, dimensions={0} | all-to-all | bytes 524288 | tf_op jit(solution)/shard_map/all_to_all | solution.py:76
  135.7 0.1 copy.110
  136.0 2.5 fusion.6
  138.4 2.3 fusion.8
  140.7 0.7 fusion.56
  141.6 2.3 fusion.59
  144.0 0.2 pad_maximum_fusion.1
  144.2 13.0 %copy.71 = bf16[4,2,16384]{0,1,2:T(2,128)(2,1)} copy(bf16[4,2,16384]{2,0,1:T(4,128)(2,1)S(1)} %pad_maximum_fusion.1) | data formatting | bytes 524288 | tf_op jit(solution)/shard_map/stack | solution.py:90
  157.1 16.8 %reshape.103 = bf16[16,2,4096]{2,1,0:T(2,128)(2,1)} reshape(bf16[16384,2,4]{2,1,0:T(2,128)(2,1)} %bitcast.136) | data formatting | bytes 524288
  173.9 6.1 %all-to-all-start.2 = ((bf16[16,2,4096]{2,1,0:T(2,128)(2,1)}), bf16[16,2,4096]{2,1,0:T(2,128)(2,1)S(1)}, u32[]{:S(2)}, u32[]{:S(2)}) async-start(bf16[16,2,4096]{2,1,0:T(2,128)(2,1)} %reshape.103), calls=%async_computation.2 | async-start | bytes 524288 | tf_op jit(solution)/shard_map/all_to_all | solution.py:91
  180.1 7.9 %all-to-all-done.2 = bf16[16,2,4096]{2,1,0:T(2,128)(2,1)S(1)} async-done(((bf16[16,2,4096]{2,1,0:T(2,128)(2,1)}), bf16[16,2,4096]{2,1,0:T(2,128)(2,1)S(1)}, u32[]{:S(2)}, u32[]{:S(2)}) %all-to-all-start.2) | async-done | bytes 262176 | tf_op jit(solution)/shard_map/all_to_all | solution.py:91
  187.9 19.0 %reshape.104 = bf16[16384,2,4]{2,1,0:T(2,128)(2,1)} reshape(bf16[16,2,4096]{2,1,0:T(2,128)(2,1)S(1)} %all-to-all-done.2) | data formatting | bytes 524288
  207.0 11.9 %copy.83 = bf16[4,2,16,1024]{3,2,1,0:T(8,128)(2,1)S(1)} copy(bf16[4,2,16,1024]{0,1,3,2:T(2,128)(2,1)} %bitcast.137) | data formatting | bytes 524288 | tf_op jit(solution)/shard_map/all_to_all | solution.py:91
  218.9 0.3 copy.73
  219.1 0.4 fusion.126
  219.5 3.1 fusion.73
  222.7 4.1 fusion
  226.8 2.5 fusion.62
  229.3 2.5 fusion.63
  231.9 0.3 copy.75
  232.2 13.0 %all_to_all.115 = bf16[64,2,1024]{2,1,0:T(2,128)(2,1)S(1)} all-to-all(bf16[64,2,1024]{2,1,0:T(2,128)(2,1)S(1)} %copy.75), channel_id=1, replica_groups=mesh['groups'=2,'freq'=16] {'freq'}, dimensions={0} | all-to-all | bytes 524288 | tf_op jit(solution)/shard_map/all_to_all | solution.py:76
  245.2 0.1 copy.109
  245.5 2.5 fusion.41
  247.9 2.3 fusion.38
  250.2 0.7 fusion.50
  251.1 2.3 fusion.53
  253.5 0.2 pad_maximum_fusion.3
  253.7 13.0 %copy.77 = bf16[4,2,16384]{0,1,2:T(2,128)(2,1)} copy(bf16[4,2,16384]{2,0,1:T(4,128)(2,1)S(1)} %pad_maximum_fusion.3) | data formatting | bytes 524288 | tf_op jit(solution)/shard_map/stack | solution.py:90
  266.6 16.2 %reshape.105 = bf16[16,2,4096]{2,1,0:T(2,128)(2,1)S(1)} reshape(bf16[16384,2,4]{2,1,0:T(2,128)(2,1)} %bitcast.138) | data formatting | bytes 524288
  282.8 12.8 %all_to_all.116 = bf16[16,2,4096]{2,1,0:T(2,128)(2,1)S(1)} all-to-all(bf16[16,2,4096]{2,1,0:T(2,128)(2,1)S(1)} %reshape.105), channel_id=1, replica_groups=mesh['groups'=2,'freq'=16] {'freq'}, dimensions={0} | all-to-all | bytes 524288 | tf_op jit(solution)/shard_map/all_to_all | solution.py:91
  295.6 6.5 %all-to-all-start.3 = ((bf16[16,128,1024]{2,1,0:T(8,128)(2,1)}), bf16[16,128,1024]{2,1,0:T(8,128)(2,1)}, u32[]{:S(2)}, u32[]{:S(2)}) async-start(bf16[16,128,1024]{2,1,0:T(8,128)(2,1)} %bitcast.141), calls=%async_computation.3 | async-start | bytes 8388608 | tf_op jit(solution)/shard_map/all_to_all | solution.py:35
  302.1 19.1 %reshape.106 = bf16[16384,2,4]{2,1,0:T(2,128)(2,1)} reshape(bf16[16,2,4096]{2,1,0:T(2,128)(2,1)S(1)} %all_to_all.116) | data formatting | bytes 524288
  321.2 11.9 %copy.84 = bf16[4,2,16,1024]{3,2,1,0:T(8,128)(2,1)S(1)} copy(bf16[4,2,16,1024]{0,1,3,2:T(2,128)(2,1)} %bitcast.139) | data formatting | bytes 524288 | tf_op jit(solution)/shard_map/all_to_all | solution.py:91
  333.1 0.3 copy.79
  333.4 0.4 fusion.125
  333.7 3.1 fusion.72
  336.9 4.9 fusion.1
  341.8 52.8 %all-to-all-done.3 = bf16[16,128,1024]{2,1,0:T(8,128)(2,1)} async-done(((bf16[16,128,1024]{2,1,0:T(8,128)(2,1)}), bf16[16,128,1024]{2,1,0:T(8,128)(2,1)}, u32[]{:S(2)}, u32[]{:S(2)}) %all-to-all-start.3) | async-done | bytes 4194336 | tf_op jit(solution)/shard_map/all_to_all | solution.py:35
  394.6 5.2 %all-to-all-start.6 = ((bf16[16,128,1024]{2,1,0:T(8,128)(2,1)}), bf16[16,128,1024]{2,1,0:T(8,128)(2,1)}, u32[]{:S(2)}, u32[]{:S(2)}) async-start(bf16[16,128,1024]{2,1,0:T(8,128)(2,1)} %bitcast.142), calls=%async_computation.6 | async-start | bytes 8388608 | tf_op jit(solution)/shard_map/all_to_all | solution.py:35
  399.8 6.5 %copy.74 = bf16[128,16,1024]{2,1,0:T(8,128)(2,1)} copy(bf16[128,16,1024]{2,0,1:T(8,128)(2,1)} %bitcast.28) | data formatting | bytes 8388608 | tf_op jit(solution)/shard_map/all_to_all | solution.py:35
  406.4 7.1 %reshape.95 = bf16[128,32,512]{2,1,0:T(8,128)(2,1)} reshape(bf16[128,16,1024]{2,1,0:T(8,128)(2,1)} %copy.74) | data formatting | bytes 8388608 | tf_op jit(solution)/shard_map/reshape | solution.py:109
  413.4 78.7 %all-to-all-done.6 = bf16[16,128,1024]{2,1,0:T(8,128)(2,1)} async-done(((bf16[16,128,1024]{2,1,0:T(8,128)(2,1)}), bf16[16,128,1024]{2,1,0:T(8,128)(2,1)}, u32[]{:S(2)}, u32[]{:S(2)}) %all-to-all-start.6) | async-done | bytes 4194336 | tf_op jit(solution)/shard_map/all_to_all | solution.py:35
  492.2 3.2 convert_bitcast_fusion
  495.4 8.3 %copy.80 = f32[128,16,1024]{2,1,0:T(8,128)} copy(f32[128,16,1024]{2,0,1:T(8,128)S(1)} %convert_bitcast_fusion) | data formatting | bytes 16777216 | tf_op jit(solution)/shard_map/convert_element_type | solution.py:108
  503.6 9.4 %reshape.97 = f32[128,32,512]{2,1,0:T(8,128)} reshape(f32[128,16,1024]{2,1,0:T(8,128)} %copy.80) | data formatting | bytes 16777216 | tf_op jit(solution)/shard_map/convert_element_type | solution.py:108
  513.0 10.2 %convert_add_fusion = f32[128,32,512]{2,1,0:T(8,128)} fusion(f32[128,32,512]{2,1,0:T(8,128)} %reshape.97, bf16[128,32,512]{2,1,0:T(8,128)(2,1)} %param.8), kind=kLoop, calls=%fused_computation.5 | loop fusion | flops 4194304 | bytes 20971520 | tf_op jit(solution)/shard_map/add | solution.py:108
  (40 shorter events, 1.1 us)
Async XLA Ops:
  8.5 6.7 %copy-start.4 = (f32[4,4]{1,0:T(4,128)S(1)}, f32[4,4]{1,0:T(4,128)}, u32[]{:S(2)}) copy-start(f32[4,4]{1,0:T(4,128)} %param.6) | copy-start | bytes 196
  8.5 25.4 %copy-start.7 = (u32[32]{0:T(128)S(1)}, u32[32]{0:T(128)}, u32[]{:S(2)}) copy-start(u32[32]{0:T(128)} %constant.74) | copy-start | bytes 388
  8.5 77.7 %copy-start.6 = (s32[4]{0:T(128)S(1)}, s32[4]{0:T(128)}, u32[]{:S(2)}) copy-start(s32[4]{0:T(128)} %param.7) | copy-start | bytes 52
  8.5 99.6 %all-to-all-start = ((bf16[128,16,1024]{0,2,1:T(8,128)(2,1)}), bf16[128,16,1024]{0,2,1:T(8,128)(2,1)}, u32[]{:S(2)}, u32[]{:S(2)}) async-start(bf16[128,16,1024]{0,2,1:T(8,128)(2,1)} %bitcast.140), calls=%async_computation | async-start | bytes 8388608 | tf_op jit(solution)/shard_map/all_to_all | solution.py:31
  15.2 1.4 collective-permute-start
  16.6 16.9 %collective-permute-start.1 = (f32[2,4,4]{2,1,0:T(4,128)S(1)}, f32[2,4,4]{2,1,0:T(4,128)S(1)}, u32[]{:S(2)}, u32[]{:S(2)}) collective-permute-start(f32[2,4,4]{2,1,0:T(4,128)S(1)} %get-tuple-element.7), channel_id=1, source_target_pairs={{0,2},{1,3},{2,0},{3,1},{4,6},{5,7},{6,4},{7,5},{8,10},{9,11},{10,... | collective-permute-start | bytes 392 | tf_op jit(solution)/shard_map/ppermute | solution.py:19
  33.5 51.8 %collective-permute-start.2 = (f32[4,4,4]{2,1,0:T(4,128)S(1)}, f32[4,4,4]{2,1,0:T(4,128)S(1)}, u32[]{:S(2)}, u32[]{:S(2)}) collective-permute-start(f32[4,4,4]{2,1,0:T(4,128)S(1)} %bitcast.155), channel_id=1, source_target_pairs={{0,4},{1,5},{2,6},{3,7},{4,0},{5,1},{6,2},{7,3},{8,12},{9,13},{10,... | collective-permute-start | bytes 776 | tf_op jit(solution)/shard_map/ppermute | solution.py:19
  85.4 20.6 %collective-permute-start.3 = (f32[8,4,4]{0,2,1:T(4,128)S(1)}, f32[8,4,4]{0,2,1:T(4,128)S(1)}, u32[]{:S(2)}, u32[]{:S(2)}) collective-permute-start(f32[8,4,4]{0,2,1:T(4,128)S(1)} %copy.82), channel_id=1, source_target_pairs={{0,8},{1,9},{2,10},{3,11},{4,12},{5,13},{6,14},{7,15},{8,0},{9,1},... | collective-permute-start | bytes 1544 | tf_op jit(solution)/shard_map/ppermute | solution.py:19
  114.5 4.5 copy-start.3
  136.0 4.8 copy-start
  173.9 14.0 %all-to-all-start.2 = ((bf16[16,2,4096]{2,1,0:T(2,128)(2,1)}), bf16[16,2,4096]{2,1,0:T(2,128)(2,1)S(1)}, u32[]{:S(2)}, u32[]{:S(2)}) async-start(bf16[16,2,4096]{2,1,0:T(2,128)(2,1)} %reshape.103), calls=%async_computation.2 | async-start | bytes 524288 | tf_op jit(solution)/shard_map/all_to_all | solution.py:91
  219.5 3.1 copy-start.5
  226.8 5.1 copy-start.2
  245.4 4.8 copy-start.1
  295.6 99.0 %all-to-all-start.3 = ((bf16[16,128,1024]{2,1,0:T(8,128)(2,1)}), bf16[16,128,1024]{2,1,0:T(8,128)(2,1)}, u32[]{:S(2)}, u32[]{:S(2)}) async-start(bf16[16,128,1024]{2,1,0:T(8,128)(2,1)} %bitcast.141), calls=%async_computation.3 | async-start | bytes 8388608 | tf_op jit(solution)/shard_map/all_to_all | solution.py:35
  394.6 97.6 %all-to-all-start.6 = ((bf16[16,128,1024]{2,1,0:T(8,128)(2,1)}), bf16[16,128,1024]{2,1,0:T(8,128)(2,1)}, u32[]{:S(2)}, u32[]{:S(2)}) async-start(bf16[16,128,1024]{2,1,0:T(8,128)(2,1)} %bitcast.142), calls=%async_computation.6 | async-start | bytes 8388608 | tf_op jit(solution)/shard_map/all_to_all | solution.py:35
